TPU v7x, 32 devices: a whole 2x2x4 slice. The times are simulated.
32 devices in a mesh: seq: 8 (over z, y), dp: 4 (over x, core).
Axes of the slice: x: 2, y: 2, z: 4, core: 2. Of those that a mesh axis runs over, the one named last changes fastest.
Arguments:
- tokens: bfloat16 [4, 2048, 2048], P('dp', 'seq'), may hold values from -6 to 6
- query_weight: bfloat16 [2048, 2048], P(None, 'seq'), may hold values from -0.125 to 0.125
- key_rows: bfloat16 [4, 2048, 2048], P('dp', 'seq'), may hold values from -6 to 6
- value_rows: bfloat16 [4, 2048, 2048], P('dp', 'seq'), may hold values from -6 to 6
- out_grad: bfloat16 [4, 2048, 2048], P('dp', 'seq'), may hold values from -6 to 6
Outputs:
- attended: bfloat16 [4, 2048, 2048], P('dp', 'seq')
- key_grad: bfloat16 [4, 2048, 2048], P('dp', 'seq')
- value_grad: bfloat16 [4, 2048, 2048], P('dp', 'seq')
- weight_grad: float32 [2048, 2048], P('seq')
All inputs are finite; a program needn't handle non-finite values.
Results may differ from a plain program's by a relative error of at most 0.0058.
Values may be sent and summed in bfloat16 or wider, within the bound.
No kernel may reach another device: no remote copies, remote signals or barrier semaphores. Data moves between devices by JAX's collectives and lax.ppermute only.
A program may use at most 320 MiB of HBM per device.

v0:
```python
import math
import jax
import jax.numpy as jnp
from jax import lax
from jax.sharding import PartitionSpec as P

DH = 128


def carried_in(value, axis, join, neutral, backward):
    count, mine = (lax.axis_size(axis), lax.axis_index(axis))
    pieces = lax.all_gather(value, axis)
    if backward:
        pieces = pieces[::-1]
        mine = count - 1 - mine
    total = jnp.full_like(value, 0) + jnp.asarray(neutral, value.dtype)

    def step(position, total):
        longer = join(total, pieces[position])
        return jnp.where(position < mine, longer, total)

    return lax.fori_loop(0, count - 1, step, total)


def pair_sum(earlier, later):
    return jax.tree.map(jnp.add, earlier, later)


def body(tokens, query_weight, key_rows, value_rows, out_grad):
    row_count = tokens.shape[1]
    hidden_width = key_rows.shape[2]
    head_count = hidden_width // DH
    seq_count = lax.axis_size("seq")
    factor = 1.0 / math.sqrt(DH * row_count * seq_count)
    local_tokens = tokens[0]
    query_rows = jnp.dot(
        local_tokens,
        lax.all_gather(query_weight, "seq", axis=1, tiled=True),
        preferred_element_type=jnp.float32,
    ).astype(jnp.bfloat16)
    query_heads = query_rows.reshape(row_count, head_count, DH)
    key_heads = key_rows[0].reshape(row_count, head_count, DH)
    value_heads = value_rows[0].reshape(row_count, head_count, DH)
    grad_heads = out_grad[0].reshape(row_count, head_count, DH)
    block_kv = jnp.einsum(
        "rhd,rhe->hde", key_heads, value_heads, preferred_element_type=jnp.float32
    )
    block_qg = jnp.einsum(
        "rhd,rhe->hde", query_heads, grad_heads, preferred_element_type=jnp.float32
    )
    zero_state = jnp.zeros_like(block_kv)
    prefix_state = carried_in(block_kv, "seq", pair_sum, zero_state, False)
    suffix_state = carried_in(block_qg, "seq", pair_sum, zero_state, True)
    prefix_half = prefix_state.astype(jnp.bfloat16)
    suffix_half = suffix_state.astype(jnp.bfloat16)
    lower_mask = (
        lax.broadcasted_iota(jnp.int32, (row_count, row_count), 0)
        >= lax.broadcasted_iota(jnp.int32, (row_count, row_count), 1)
    )[None]
    key_scores = jnp.where(
        lower_mask,
        factor
        * jnp.einsum("ihd,jhd->hij", query_heads, key_heads, preferred_element_type=jnp.float32),
        0.0,
    ).astype(jnp.bfloat16)
    grad_scores = jnp.where(
        lower_mask,
        factor
        * jnp.einsum("ihe,jhe->hij", grad_heads, value_heads, preferred_element_type=jnp.float32),
        0.0,
    ).astype(jnp.bfloat16)
    attended = jnp.einsum(
        "hij,jhe->ihe", key_scores, value_heads, preferred_element_type=jnp.float32
    ) + factor * jnp.einsum(
        "ihd,hde->ihe", query_heads, prefix_half, preferred_element_type=jnp.float32
    )
    query_grad = jnp.einsum(
        "hij,jhd->ihd", grad_scores, key_heads, preferred_element_type=jnp.float32
    ) + factor * jnp.einsum(
        "ihe,hde->ihd", grad_heads, prefix_half, preferred_element_type=jnp.float32
    )
    key_grad = jnp.einsum(
        "hij,ihd->jhd", grad_scores, query_heads, preferred_element_type=jnp.float32
    ) + factor * jnp.einsum(
        "jhe,hde->jhd", value_heads, suffix_half, preferred_element_type=jnp.float32
    )
    value_grad = jnp.einsum(
        "hij,ihe->jhe", key_scores, grad_heads, preferred_element_type=jnp.float32
    ) + factor * jnp.einsum(
        "jhd,hde->jhe", key_heads, suffix_half, preferred_element_type=jnp.float32
    )
    attended = attended.reshape(1, row_count, hidden_width).astype(jnp.bfloat16)
    query_grad = query_grad.reshape(row_count, hidden_width).astype(jnp.bfloat16)
    key_grad = key_grad.reshape(1, row_count, hidden_width).astype(jnp.bfloat16)
    value_grad = value_grad.reshape(1, row_count, hidden_width).astype(jnp.bfloat16)
    grad_shard = lax.psum_scatter(
        lax.dot_general(
            local_tokens, query_grad, (((0,), (0,)), ((), ())), preferred_element_type=jnp.float32
        ),
        "seq",
        scatter_dimension=0,
        tiled=True,
    )
    weight_grad = lax.psum(grad_shard, "dp")
    return (attended, key_grad, value_grad, weight_grad)


def solution(mesh):
    return jax.shard_map(
        body,
        mesh=mesh,
        in_specs=(
            P("dp", "seq", None),
            P(None, "seq"),
            P("dp", "seq", None),
            P("dp", "seq", None),
            P("dp", "seq", None),
        ),
        out_specs=(
            P("dp", "seq", None),
            P("dp", "seq", None),
            P("dp", "seq", None),
            P("seq", None),
        ),
        check_vma=False,
    )
```

profile of v0, /device:TPU:0, one launch (start us, length us, event | category | flops | bytes accessed | tf_op | source)
XLA Modules:
  0.0 732.2 jit_solution(10739160041827640124)
XLA Ops:
  7.2 0.0 copy-start
  7.2 0.0 all-gather.6.cloned.1.call-start
  7.2 0.7 all-gather.6.cloned.1.call-update
  7.9 0.0 all-gather.8.cloned.1.call-start
  8.0 1.5 copy.57
  9.4 1.2 copy.56
  10.7 1.6 copy.34
  12.3 1.4 fusion.17
  13.7 0.0 all-gather.8.cloned.1.call-update
  13.8 0.0 all-gather.10.cloned.1.call-start
  13.8 2.5 copy.58
  16.3 121.4 %all-gather.6.cloned.1.call-done = bf16[2048,2048]{1,0:T(8,128)(2,1)} async-done(((bf16[2048,256]{1,0:T(8,128)(2,1)}), bf16[2048,2048]{1,0:T(8,128)(2,1)}) %all-gather.6.cloned.1.call-update) | async-done | bytes 8388624 | tf_op jit(solution)/shard_map/all_gather | solution.py:38
  137.7 6.7 convolution_convert_fusion
  144.4 1.5 copy.55
  145.9 0.0 copy-start.2
  145.9 3.2 fusion.11
  149.2 0.0 all-gather.10.cloned.1.call-update
  149.2 0.0 reduce-scatter.2.cloned.1.call-start
  149.3 0.0 copy-start.7
  149.3 2.1 select_convert_fusion
  151.5 1.3 copy-done.11
  152.8 2.2 fusion.24
  155.0 108.1 %all-gather.8.cloned.1.call-done = f32[128,128,128]{2,1,0:T(8,128)} async-done(((f32[16,128,128]{2,1,0:T(8,128)}), f32[128,128,128]{2,1,0:T(8,128)}) %all-gather.8.cloned.1.call-update) | async-done | bytes 8388624 | tf_op jit(solution)/shard_map/all_gather | solution.py:12
  263.1 11.6 %while.28 = (s32[]{:T(128)}, f32[16,128,128]{2,1,0:T(8,128)S(1)}, s32[]{:T(128)}, f32[8,16,128,128]{3,2,1,0:T(8,128)}, s32[]{:T(128)}, /*index=5*/s32[]{:T(128)}) while((s32[]{:T(128)}, f32[16,128,128]{2,1,0:T(8,128)S(1)}, s32[]{:T(128)}, f32[8,16,128,128]{3,2,1,0:T(8,128)}, s32[]{:T(128)}, /*index=5*/s32[]{:T(128)}) %tuple.81), condition=%wide.region_1.2_spmd.clone, body=%wide.region_0.1_spmd.clone.sunk | while | flops 786436 | bytes 3145821 | solution.py:22
  263.1 1.6 add_select_fusion.4
  264.7 1.6 add_select_fusion.4
  266.3 1.6 add_select_fusion.4
  268.0 1.6 add_select_fusion.4
  269.6 1.7 add_select_fusion.4
  271.3 1.7 add_select_fusion.4
  273.0 1.7 add_select_fusion.4
  274.8 2.4 fusion
  277.2 8.1 %convolution_bitcast_fusion = f32[2048,2048]{0,1:T(8,128)} fusion(bf16[256,2048]{0,1:T(8,128)(2,1)S(1)} %bitcast.79, bf16[1,256,2048]{2,1,0:T(8,128)(2,1)S(1)} %copy-done), kind=kOutput, calls=%fused_computation.2 | convolution fusion | flops 2147483648 | bytes 18874368 | tf_op jit(solution)/shard_map/dot_general | solution.py:97
  285.3 0.0 reduce-scatter.2.cloned.1.call-update
  285.3 0.2 all-reduce.2.cloned.1.call-start
  285.6 2.4 select_convert_fusion.1
  288.0 0.8 fusion.13
  288.9 0.5 copy-done.9
  289.4 0.6 copy-done.3
  290.0 1.5 fusion.2
  291.5 2.4 copy.49
  293.8 3.4 fusion.23
  297.2 90.8 %all-gather.10.cloned.1.call-done = f32[128,128,128]{2,1,0:T(8,128)} async-done(((f32[16,128,128]{2,1,0:T(8,128)}), f32[128,128,128]{2,1,0:T(8,128)}) %all-gather.10.cloned.1.call-update) | async-done | bytes 8388624 | tf_op jit(solution)/shard_map/all_gather | solution.py:12
  387.9 7.7 %rev.3 = f32[8,16,128,128]{3,2,1,0:T(8,128)} reverse(f32[8,16,128,128]{3,2,1,0:T(8,128)} %bitcast.78), dimensions={0} | reverse | bytes 16777216 | tf_op jit(solution)/shard_map/rev | solution.py:14
  395.7 11.4 %while.29 = (s32[]{:T(128)}, f32[16,128,128]{2,1,0:T(8,128)S(1)}, s32[]{:T(128)}, f32[8,16,128,128]{3,2,1,0:T(8,128)}, s32[]{:T(128)}, /*index=5*/s32[]{:T(128)}) while((s32[]{:T(128)}, f32[16,128,128]{2,1,0:T(8,128)S(1)}, s32[]{:T(128)}, f32[8,16,128,128]{3,2,1,0:T(8,128)}, s32[]{:T(128)}, /*index=5*/s32[]{:T(128)}) %tuple.68), condition=%wide.region_3.4_spmd.clone, body=%wide.region_2.3_spmd.clone.sunk | while | flops 786436 | bytes 3145821 | solution.py:22
  395.7 1.6 add_select_fusion.5
  397.3 1.6 add_select_fusion.5
  399.0 1.6 add_select_fusion.5
  400.6 1.6 add_select_fusion.5
  402.2 1.6 add_select_fusion.5
  403.8 1.6 add_select_fusion.5
  405.5 1.6 add_select_fusion.5
  407.1 263.0 %reduce-scatter.2.cloned.1.call-done = f32[256,2048]{0,1:T(8,128)} async-done(((f32[2048,2048]{0,1:T(8,128)}), f32[256,2048]{0,1:T(8,128)}) %reduce-scatter.2.cloned.1.call-update) | async-done | bytes 2097168 | tf_op jit(solution)/shard_map/reduce_scatter | solution.py:96
  670.1 0.0 all-reduce.2.cloned.1.call-update
  670.1 3.1 add_convert_fusion
  673.2 2.4 copy.50
  675.5 0.5 fusion.5
  676.0 0.7 copy-done.5
  676.8 1.0 copy-done.10
  677.8 0.6 fusion.1
  678.4 0.0 copy-start.1
  678.4 1.4 copy.51
  679.9 43.0 %all-reduce.2.cloned.1.call-done = f32[256,2048]{0,1:T(8,128)} async-done(((f32[256,2048]{0,1:T(8,128)}), f32[256,2048]{0,1:T(8,128)}) %all-reduce.2.cloned.1.call-update) | async-done | bytes 2097168 | tf_op jit(solution)/shard_map/psum | solution.py:104
  722.8 2.9 copy.52
  (20 shorter events, 0.1 us)
Async XLA Ops:
  7.2 130.6 %copy-start = (bf16[1,256,2048]{2,1,0:T(8,128)(2,1)S(1)}, bf16[1,256,2048]{2,1,0:T(8,128)(2,1)}, u32[]{:S(2)}) copy-start(bf16[1,256,2048]{2,1,0:T(8,128)(2,1)} %param.9) | copy-start | bytes 3145732
  7.2 2.3 copy-start.12
  7.2 130.5 %all-gather.6.cloned.1.call-start = ((), (), s32[]{:S(2)}) async-start(), calls=%async_computation.1 | async-start | bytes 9437184 | tf_op jit(solution)/shard_map/all_gather | solution.py:38
  7.9 255.2 %all-gather.8.cloned.1.call-start = ((), (), s32[]{:S(2)}) async-start(), calls=%async_computation.4 | async-start | bytes 9437184 | tf_op jit(solution)/shard_map/all_gather | solution.py:12
  12.3 1.5 copy-start.6
  13.8 374.2 %all-gather.10.cloned.1.call-start = ((), (), s32[]{:S(2)}) async-start(), calls=%async_computation.5 | async-start | bytes 9437184 | tf_op jit(solution)/shard_map/all_gather | solution.py:12
  145.9 3.3 copy-start.2
  149.2 520.9 %reduce-scatter.2.cloned.1.call-start = ((), (), s32[]{:S(2)}) async-start(), calls=%async_computation.2 | async-start | bytes 18874368 | tf_op jit(solution)/shard_map/reduce_scatter | solution.py:96
  149.3 3.5 copy-start.7
  151.5 1.3 copy-start.11
  285.3 437.5 %all-reduce.2.cloned.1.call-start = ((), (), s32[]{:S(2)}) async-start(), calls=%async_computation.3 | async-start | bytes 4194304 | tf_op jit(solution)/shard_map/psum | solution.py:104
  288.0 1.4 copy-start.9
  288.0 2.0 copy-start.3
  291.5 2.4 copy-start.4
  673.2 2.4 copy-start.8
  675.5 1.3 copy-start.5
  675.5 2.3 copy-start.10
  678.4 47.3 %copy-start.1 = (bf16[1,256,2048]{2,1,0:T(8,128)(2,1)S(1)}, bf16[1,256,2048]{2,1,0:T(8,128)(2,1)}, u32[]{:S(2)}) copy-start(bf16[1,256,2048]{2,1,0:T(8,128)(2,1)} %param.9) | copy-start | bytes 3145732
Sparse Core Ops, SparseCore 0:
  10.0 127.6 all-gather.5
  140.4 122.6 all-gather.7
  265.3 122.6 all-gather.9
  391.6 278.4 reduce-scatter.1
  672.3 50.4 all-reduce.1
where the time goes:
time: 733 us; the launch traced here: 732 us
  waiting for transfers between devices  627 us (86%)
  matrix products  38.5 us (5%)
  local copies, waits for them, and re-layouts  29.3 us (4%)
  other arithmetic  22.7 us (3%)
  between operations  14 us (2%)
    reduce_scatter x1, waiting for transfers between devices, body(): lax.psum_scatter(lax.dot_general(local_tokens, query_grad, (((0,), (0,)),...  263 us
    all_gather x2, waiting for transfers between devices, carried_in(): pieces = lax.all_gather(value, axis)  199 us
    all_gather x1, waiting for transfers between devices, body(): lax.all_gather(query_weight, 'seq', axis=1, tiled=True)  121 us
    psum x1, waiting for transfers between devices, body(): weight_grad = lax.psum(grad_shard, 'dp')  43 us
    select_n x14, other arithmetic, step(): return jnp.where(position < mine, longer, total)  22.7 us
    unnamed x33, local copies, waits for them, and re-layouts  18.5 us
  transfers between devices with their start and end apart: 5, of which 5 were waited for; matrix products, arithmetic and copies ran while one was open for 11% of the time, Pallas kernels for 0%

commit v1 on v0

--- a/solution.py
+++ b/solution.py
@@ -5,6 +5,15 @@
 from jax.sharding import PartitionSpec as P
 
 DH = 128
+
+
+def _derive_sections(vector):
+    n = lax.axis_size("dp")
+    before = vector
+    for idx in [[(rr, rr ^ no) for rr in range(n)] for no in (1, 2, 4, 8, 16) if no < n]:
+        current_value = lax.ppermute(before, "dp", idx)
+        before = before + current_value
+    return before
 
 
 def carried_in(value, axis, join, neutral, backward):
@@ -101,7 +110,7 @@
         scatter_dimension=0,
         tiled=True,
     )
-    weight_grad = lax.psum(grad_shard, "dp")
+    weight_grad = _derive_sections(grad_shard)
     return (attended, key_grad, value_grad, weight_grad)
 
 

time: 733 us -> 747 us (1.019)
  other arithmetic: 22.7 us -> 30.3 us
    psum x1 -> x0, waiting for transfers between devices: 43 us -> none  [body(): weight_grad = lax.psum(grad_shard, 'dp')]
    all_gather x2, waiting for transfers between devices: 199 us -> 232 us  [carried_in(): pieces = lax.all_gather(value, axis)]
    ppermute x0 -> x2, waiting for transfers between devices: none -> 24.8 us  [_derive_sections(): current_value = lax.ppermute(before, 'dp', idx)]
    all_gather x1, waiting for transfers between devices: 121 us -> 103 us  [body(): lax.all_gather(query_weight, 'seq', axis=1, tiled=True)]
    add x0 -> x2, other arithmetic: none -> 7.72 us  [_derive_sections(): before = before + current_value]
    reduce_scatter x1, waiting for transfers between devices: 263 us -> 271 us  [body(): lax.psum_scatter(lax.dot_general(local_tokens, query_grad, (((0,), (0,)),...]
  transfers between devices with their start and end apart: 5 -> 6, of which waited for: 5 -> 5; matrix products, arithmetic and copies ran while one was open for 11% -> 10% of each run, Pallas kernels for 0% -> 0%
where the time goes in v1:
time: 747 us; the launch traced here: 745 us
  waiting for transfers between devices  631 us (84%)
  matrix products  38.9 us (5%)
  other arithmetic  30.3 us (4%)
  local copies, waits for them, and re-layouts  29 us (4%)
  between operations  14 us (2%)
    reduce_scatter x1, waiting for transfers between devices, body(): lax.psum_scatter(lax.dot_general(local_tokens, query_grad, (((0,), (0,)),...  271 us
    all_gather x2, waiting for transfers between devices, carried_in(): pieces = lax.all_gather(value, axis)  232 us
    all_gather x1, waiting for transfers between devices, body(): lax.all_gather(query_weight, 'seq', axis=1, tiled=True)  103 us
    ppermute x2, waiting for transfers between devices, _derive_sections(): current_value = lax.ppermute(before, 'dp', idx)  24.8 us
    select_n x14, other arithmetic, step(): return jnp.where(position < mine, longer, total)  22.5 us
    unnamed x33, local copies, waits for them, and re-layouts  18.2 us
  transfers between devices with their start and end apart: 6, of which 5 were waited for; matrix products, arithmetic and copies ran while one was open for 10% of the time, Pallas kernels for 0%

profile of v1, /device:TPU:0, one launch (start us, length us, event | category | flops | bytes accessed | tf_op | source)
XLA Modules:
  0.0 745.5 jit_solution(2825717203893851360)
XLA Ops:
  7.2 0.0 copy-start
  7.2 0.0 all-gather.8.cloned.1.call-start
  7.2 1.6 copy.57
  8.8 1.2 copy.56
  10.1 1.6 copy.34
  11.7 0.0 copy-start.6
  11.7 1.4 fusion.17
  13.1 0.0 all-gather.8.cloned.1.call-update
  13.2 0.0 all-gather.6.cloned.1.call-start
  13.2 0.7 all-gather.6.cloned.1.call-update
  13.9 0.0 reduce-scatter.2.cloned.1.call-start
  14.0 2.5 copy.58
  16.5 0.0 copy-start.7
  16.5 2.1 select_convert_fusion
  18.6 1.3 copy-done.11
  20.0 2.2 fusion.24
  22.2 118.3 %all-gather.8.cloned.1.call-done = f32[128,128,128]{2,1,0:T(8,128)} async-done(((f32[16,128,128]{2,1,0:T(8,128)}), f32[128,128,128]{2,1,0:T(8,128)}) %all-gather.8.cloned.1.call-update) | async-done | bytes 8388624 | tf_op jit(solution)/shard_map/all_gather | solution.py:21
  140.5 11.5 %while.28 = (s32[]{:T(128)}, f32[16,128,128]{2,1,0:T(8,128)S(1)}, s32[]{:T(128)}, f32[8,16,128,128]{3,2,1,0:T(8,128)}, s32[]{:T(128)}, /*index=5*/s32[]{:T(128)}) while((s32[]{:T(128)}, f32[16,128,128]{2,1,0:T(8,128)S(1)}, s32[]{:T(128)}, f32[8,16,128,128]{3,2,1,0:T(8,128)}, s32[]{:T(128)}, /*index=5*/s32[]{:T(128)}) %tuple.79), condition=%wide.region_1.2_spmd.clone, body=%wide.region_0.1_spmd.clone.sunk | while | flops 786436 | bytes 3145821 | solution.py:31
  140.5 1.6 add_select_fusion.4
  142.1 1.6 add_select_fusion.4
  143.8 1.6 add_select_fusion.4
  145.4 1.6 add_select_fusion.4
  147.0 1.7 add_select_fusion.4
  148.7 1.7 add_select_fusion.4
  150.4 1.6 add_select_fusion.4
  152.1 2.5 fusion
  154.6 8.1 %convolution_bitcast_fusion = f32[2048,2048]{0,1:T(8,128)} fusion(bf16[256,2048]{0,1:T(8,128)(2,1)S(1)} %bitcast.79, bf16[1,256,2048]{2,1,0:T(8,128)(2,1)S(1)} %copy-done), kind=kOutput, calls=%fused_computation.2 | convolution fusion | flops 2147483648 | bytes 18874368 | tf_op jit(solution)/shard_map/dot_general | solution.py:106
  162.6 0.0 reduce-scatter.2.cloned.1.call-update
  162.6 0.2 all-gather.10.cloned.1.call-start
  162.9 102.8 %all-gather.6.cloned.1.call-done = bf16[2048,2048]{1,0:T(8,128)(2,1)} async-done(((bf16[2048,256]{1,0:T(8,128)(2,1)}), bf16[2048,2048]{1,0:T(8,128)(2,1)}) %all-gather.6.cloned.1.call-update) | async-done | bytes 8388624 | tf_op jit(solution)/shard_map/all_gather | solution.py:47
  265.7 6.7 convolution_convert_fusion
  272.4 1.5 copy.55
  273.9 3.3 fusion.11
  277.2 0.0 all-gather.10.cloned.1.call-update
  277.2 270.7 %reduce-scatter.2.cloned.1.call-done = f32[256,2048]{0,1:T(8,128)} async-done(((f32[2048,2048]{0,1:T(8,128)}), f32[256,2048]{0,1:T(8,128)}) %reduce-scatter.2.cloned.1.call-update) | async-done | bytes 2097168 | tf_op jit(solution)/shard_map/reduce_scatter | solution.py:105
  548.0 2.4 select_convert_fusion.1
  550.4 0.8 fusion.13
  551.3 0.5 copy-done.9
  551.8 0.6 copy-done.3
  552.4 1.5 fusion.2
  553.9 2.4 copy.49
  556.2 3.7 fusion.23
  559.9 113.7 %all-gather.10.cloned.1.call-done = f32[128,128,128]{2,1,0:T(8,128)} async-done(((f32[16,128,128]{2,1,0:T(8,128)}), f32[128,128,128]{2,1,0:T(8,128)}) %all-gather.10.cloned.1.call-update) | async-done | bytes 8388624 | tf_op jit(solution)/shard_map/all_gather | solution.py:21
  673.6 7.8 %rev.3 = f32[8,16,128,128]{3,2,1,0:T(8,128)} reverse(f32[8,16,128,128]{3,2,1,0:T(8,128)} %bitcast.78), dimensions={0} | reverse | bytes 16777216 | tf_op jit(solution)/shard_map/rev | solution.py:23
  681.3 3.8 add.81
  685.2 1.5 collective-permute-start.1
  686.6 11.3 %while.29 = (s32[]{:T(128)}, f32[16,128,128]{2,1,0:T(8,128)S(1)}, s32[]{:T(128)}, f32[8,16,128,128]{3,2,1,0:T(8,128)}, s32[]{:T(128)}, /*index=5*/s32[]{:T(128)}) while((s32[]{:T(128)}, f32[16,128,128]{2,1,0:T(8,128)S(1)}, s32[]{:T(128)}, f32[8,16,128,128]{3,2,1,0:T(8,128)}, s32[]{:T(128)}, /*index=5*/s32[]{:T(128)}) %tuple.68), condition=%wide.region_3.4_spmd.clone, body=%wide.region_2.3_spmd.clone.sunk | while | flops 786436 | bytes 3145821 | solution.py:31
  686.6 1.6 add_select_fusion.5
  688.2 1.6 add_select_fusion.5
  689.9 1.6 add_select_fusion.5
  691.5 1.6 add_select_fusion.5
  693.1 1.6 add_select_fusion.5
  694.7 1.6 add_select_fusion.5
  696.3 1.6 add_select_fusion.5
  697.9 3.1 add_convert_fusion
  701.0 2.4 copy.50
  703.4 0.5 fusion.5
  703.9 0.7 copy-done.5
  704.6 0.7 copy-done.10
  705.3 0.6 fusion.1
  705.9 1.4 copy.51
  707.3 24.8 %collective-permute-done.1 = f32[256,2048]{0,1:T(8,128)} collective-permute-done((f32[256,2048]{0,1:T(8,128)}, f32[256,2048]{0,1:T(8,128)}, u32[]{:S(2)}, u32[]{:S(2)}) %collective-permute-start.1) | collective-permute-done | bytes 2097184 | tf_op jit(solution)/shard_map/ppermute | solution.py:14
  732.1 3.9 add.82
  736.0 2.9 copy.52
  (23 shorter events, 0.1 us)
Async XLA Ops:
  7.2 147.4 %copy-start = (bf16[1,256,2048]{2,1,0:T(8,128)(2,1)S(1)}, bf16[1,256,2048]{2,1,0:T(8,128)(2,1)}, u32[]{:S(2)}) copy-start(bf16[1,256,2048]{2,1,0:T(8,128)(2,1)} %param.9) | copy-start | bytes 3145732
  7.2 1.7 copy-start.12
  7.2 133.3 %all-gather.8.cloned.1.call-start = ((), (), s32[]{:S(2)}) async-start(), calls=%async_computation.3 | async-start | bytes 9437184 | tf_op jit(solution)/shard_map/all_gather | solution.py:21
  11.7 1.5 copy-start.6
  13.2 252.5 %all-gather.6.cloned.1.call-start = ((), (), s32[]{:S(2)}) async-start(), calls=%async_computation.1 | async-start | bytes 9437184 | tf_op jit(solution)/shard_map/all_gather | solution.py:47
  13.9 534.0 %reduce-scatter.2.cloned.1.call-start = ((), (), s32[]{:S(2)}) async-start(), calls=%async_computation.2 | async-start | bytes 18874368 | tf_op jit(solution)/shard_map/reduce_scatter | solution.py:105
  16.5 3.5 copy-start.7
  18.6 1.3 copy-start.11
  162.6 510.9 %all-gather.10.cloned.1.call-start = ((), (), s32[]{:S(2)}) async-start(), calls=%async_computation.4 | async-start | bytes 9437184 | tf_op jit(solution)/shard_map/all_gather | solution.py:21
  273.9 3.3 copy-start.2
  548.0 133.4 %collective-permute-start = (f32[256,2048]{0,1:T(8,128)}, f32[256,2048]{0,1:T(8,128)}, u32[]{:S(2)}, u32[]{:S(2)}) collective-permute-start(f32[256,2048]{0,1:T(8,128)} %reduce-scatter.2.cloned.1.call-done), channel_id=1, source_target_pairs={{0,1},{1,0},{2,3},{3,2},{4,5},{5,4},{6,7},{7,6},{8,9},{9,8},{10,11... | collective-permute-start | bytes 6291464 | tf_op jit(solution)/shard_map/ppermute | solution.py:14
  550.4 1.4 copy-start.9
  550.4 2.0 copy-start.3
  553.9 2.4 copy-start.4
  685.2 47.0 %collective-permute-start.1 = (f32[256,2048]{0,1:T(8,128)}, f32[256,2048]{0,1:T(8,128)}, u32[]{:S(2)}, u32[]{:S(2)}) collective-permute-start(f32[256,2048]{0,1:T(8,128)} %add.81), channel_id=1, source_target_pairs={{0,2},{1,3},{2,0},{3,1},{4,6},{5,7},{6,4},{7,5},{8,10},{9,11},{10,... | collective-permute-start | bytes 6291464 | tf_op jit(solution)/shard_map/ppermute | solution.py:14
  701.0 2.4 copy-start.8
  703.3 1.2 copy-start.5
  703.3 1.9 copy-start.10
  732.1 6.8 copy-start.1
Sparse Core Ops, SparseCore 0:
  13.3 127.1 all-gather.7
  142.6 123.1 all-gather.5
  269.5 278.4 reduce-scatter.1
  549.9 123.5 all-gather.9
